TPU v7x, 256 devices: a whole 4x4x8 slice. The times are simulated.
256 devices in a mesh: pix: 32 (over z, y), shell: 8 (over x, core).
Axes of the slice: x: 4, y: 4, z: 8, core: 2. Of those that a mesh axis runs over, the one named last changes fastest.
Arguments:
- field: float32 [128, 1048576], P('shell', 'pix'), may hold values from -3 to 3
- momentum: float32 [128, 1048576], P('shell', 'pix'), may hold values from -6 to 6
- kernels: float32 [4, 20, 128], P(None, None, 'shell'), may hold values from 0.002 to 0.02
- depth_class: int32 [1048576], P('pix'), may hold values from 0 to 3
- counts: int32 [20, 1048576], P(None, 'pix'), may hold values from 0 to 12
- mask: float32 [1048576], P('pix'), may hold values from 0.1 to 1.5, as said below
- mean_counts: float32 [20], replicated, may hold values from 1 to 8
- shell_scale: float32 [128], P('shell'), may hold values from 0.5 to 2
Outputs:
- gradient: float32 [128, 1048576], P('shell', 'pix')
- loglik: float32 [], replicated
Inputs may be any that keep to these rules, and one draw needn't show every extreme that they name: `mask`: mask weights are positive.
All inputs are finite; a program needn't handle non-finite values.
Results may differ from a plain program's by a relative error of at most 0.00005.
Values sent between devices are 32-bit elements; how exact they have to be, the bound alone decides.
No kernel may reach another device: no remote copies, remote signals or barrier semaphores. Data moves between devices by JAX's collectives and lax.ppermute only.
A program may use at most 128 MiB of HBM per device.

v0:
```python
import jax
import jax.numpy as jnp
from jax import lax
from jax.sharding import PartitionSpec as P

CYCLE = 2048
LEAP = 0.1
ANGULAR = 0.5
RADIAL = 0.5


def padded_2(cells, sides, width):
    for axis, dim in sides:
        count = lax.axis_size(axis)
        ends = count - 1
        head = lax.slice_in_dim(cells, 0, width, axis=dim)
        tail = lax.slice_in_dim(cells, cells.shape[dim] - width, cells.shape[dim], axis=dim)
        cells = jnp.concatenate(
            [
                lax.ppermute(tail, axis, [(i, (i + 1) % count) for i in range(ends)]),
                cells,
                lax.ppermute(head, axis, [((i + 1) % count, i) for i in range(ends)]),
            ],
            axis=dim,
        )
    return cells


def shards(field, momentum, kernels, depth_class, counts, mask, mean_counts, shell_scale):
    shells_here, pixels = field.shape
    classes, bins, _ = kernels.shape
    total_pix = pixels * lax.axis_size("pix")
    position = field + LEAP * momentum
    density = jnp.exp(position)
    flat = kernels.reshape(classes * bins, shells_here)
    onehot = (depth_class[None, :] == jnp.arange(classes, dtype=jnp.int32)[:, None]).astype(
        jnp.float32
    )
    every = jnp.dot(
        flat, density, precision=lax.Precision.HIGHEST, preferred_element_type=jnp.float32
    )
    partial_proj = jnp.sum(every.reshape(classes, bins, pixels) * onehot[:, None, :], axis=0)
    counted = counts.astype(jnp.float32)
    proj = lax.psum(partial_proj, "shell")
    weighted, total = lax.psum(
        (jnp.sum(mask[None, :] * proj, axis=1), jnp.sum(counted, axis=1)), "pix"
    )
    norm = weighted / total_pix
    rate = mean_counts[:, None] * mask[None, :] * proj / norm[:, None]
    local_sum = jnp.sum(counted * jnp.log(rate) - rate)
    loglik = lax.psum(local_sum, "pix") / (bins * total_pix)
    ratio = counted / proj - (total / (total_pix * norm))[:, None] * mask[None, :]
    padded = padded_2(position, (("pix", 1),), CYCLE)
    angular = (
        4.0 * position
        - padded[:, CYCLE - 1 : CYCLE - 1 + pixels]
        - padded[:, CYCLE + 1 : CYCLE + 1 + pixels]
    )
    angular = angular - padded[:, 0:pixels] - padded[:, 2 * CYCLE : 2 * CYCLE + pixels]
    stacked = padded_2(position, (("shell", 0),), 1)
    radial = 2.0 * position - stacked[:-2] - stacked[2:]
    spread = (onehot[:, None, :] * ratio[None, :, :]).reshape(classes * bins, pixels)
    back = lax.dot_general(
        flat,
        spread,
        (((0,), (0,)), ((), ())),
        precision=lax.Precision.HIGHEST,
        preferred_element_type=jnp.float32,
    )
    like = density * back
    gradient = (
        like
        - position / (shell_scale[:, None] * shell_scale[:, None])
        - ANGULAR * angular
        - RADIAL * radial
    )
    return (gradient, loglik)


def solution(mesh):
    placed = (
        P("shell", "pix"),
        P("shell", "pix"),
        P(None, None, "shell"),
        P("pix"),
        P(None, "pix"),
        P("pix"),
        P(),
        P("shell"),
    )
    return jax.shard_map(
        shards, mesh=mesh, in_specs=placed, out_specs=(P("shell", "pix"), P()), check_vma=False
    )
```

profile of v0, /device:TPU:8, one launch (start us, length us, event | category | flops | bytes accessed | tf_op | source)
XLA Modules:
  0.0 298.6 jit_solution(3591351216382486892)
XLA Ops:
  7.2 0.0 all-reduce.3.cloned.1.call-start
  7.2 0.8 copy.10
  8.0 0.1 reshape.36
  8.1 2.5 multiply_add_fusion
  10.5 0.0 copy-start.1
  10.5 10.9 %convolution_bitcast_fusion = f32[80,32768]{1,0:T(8,128)} fusion(f32[80,16]{0,1:T(8,128)S(1)} %reshape.36, f32[16,32768]{1,0:T(8,128)S(1)} %multiply_add_fusion), kind=kOutput, calls=%fused_computation | convolution fusion | flops 503316480 | bytes 12588032 | tf_op jit(solution)/shard_map/dot_general | solution.py:39
  21.4 0.0 copy-start.4
  21.4 11.4 %reshape.37 = f32[4,20,32768]{2,1,0:T(8,128)} reshape(f32[80,32768]{1,0:T(8,128)} %convolution_bitcast_fusion) | data formatting | bytes 20971520 | tf_op jit(solution)/shard_map/reshape | solution.py:42
  32.8 0.0 copy-done.4
  32.8 0.1 fusion.20
  32.9 0.0 copy-start.2
  32.9 0.8 copy-done.2
  33.7 8.0 %multiply_reduce_fusion = f32[20,32768]{1,0:T(8,128)} fusion(f32[4,20,32768]{2,1,0:T(8,128)} %reshape.37, f32[4,32768]{1,0:T(4,128)S(1)} %fusion.20), kind=kLoop, calls=%fused_computation.5 | loop fusion | flops 4587520 | bytes 13631488 | tf_op jit(solution)/shard_map/reduce_sum | solution.py:42
  41.7 0.0 copy-start.3
  41.7 0.0 all-reduce.3.cloned.1.call-update
  41.8 0.0 copy-start.6
  41.8 0.0 copy-start.5
  41.8 3.6 %collective-permute-start = (f32[16,2048]{1,0:T(8,128)S(1)}, f32[16,2048]{1,0:T(8,128)}, u32[]{:S(2)}, u32[]{:S(2)}) collective-permute-start(f32[16,2048]{1,0:T(8,128)S(1)} %get-tuple-element.8), channel_id=1, source_target_pairs={{0,8},{8,16},{16,24},{24,32},{32,40},{40,48},{48,56},{56,64},{64,7... | collective-permute-start | bytes 393224 | tf_op jit(solution)/shard_map/ppermute | solution.py:20
  45.4 3.0 %collective-permute-start.1 = (f32[16,2048]{1,0:T(8,128)S(1)}, f32[16,2048]{1,0:T(8,128)}, u32[]{:S(2)}, u32[]{:S(2)}) collective-permute-start(f32[16,2048]{1,0:T(8,128)S(1)} %get-tuple-element.9), channel_id=1, source_target_pairs={{8,0},{16,8},{24,16},{32,24},{40,32},{48,40},{56,48},{64,56},{72,6... | collective-permute-start | bytes 393224 | tf_op jit(solution)/shard_map/ppermute | solution.py:22
  48.4 0.0 copy-done.1
  48.5 0.9 fusion.21
  49.3 1.9 collective-permute-start.2
  51.3 1.3 collective-permute-start.3
  52.6 66.3 %all-reduce.3.cloned.1.call-done = f32[20,32768]{1,0:T(8,128)} async-done(((f32[20,32768]{1,0:T(8,128)}), f32[20,32768]{1,0:T(8,128)}) %all-reduce.3.cloned.1.call-update) | async-done | bytes 2621456 | tf_op jit(solution)/shard_map/psum | solution.py:44
  118.9 0.0 copy-done.3
  118.9 0.0 copy-start
  118.9 2.4 multiply_reduce_fusion.1
  121.3 0.0 copy-done.6
  121.3 71.1 %psum.30 = f32[20]{0:T(128)S(1)} all-reduce(f32[20]{0:T(128)S(1)} %multiply_reduce_fusion.1), channel_id=1, replica_groups=mesh['pix'=32,'shell'=8] {'pix'}, use_global_device_ids=true, to_apply=%region_5.0 | all-reduce | flops 20 | bytes 160 | tf_op jit(solution)/shard_map/psum | solution.py:45
  192.5 0.0 copy-done.5
  192.5 0.0 copy-done
  192.5 3.6 %subtract_reduce_fusion = (f32[]{:T(128)}, f32[20]{0:T(128)S(1)}) fusion(f32[20,32768]{1,0:T(8,128)S(1)} %copy-done, s32[20,32768]{1,0:T(8,128)} %param.12, f32[20]{0:T(128)S(1)} %broadcast_multiply_fusion, f32[20]{0:T(128)S(1)} %copy-done.5, f32[32768]{0:T(1024)S(1)} %copy-done.3), kind=kLoop, calls=%fused_computation.8 | loop fusion | flops 5242859 | bytes 5374196 | tf_op jit(solution)/shard_map/reduce_sum | solution.py:50
  196.1 74.9 %all-reduce = (f32[20]{0:T(128)S(1)}, f32[]{:T(128)}) all-reduce(f32[20]{0:T(128)S(1)} %get-tuple-element.3, f32[]{:T(128)} %get-tuple-element.2), channel_id=1, replica_groups=mesh['pix'=32,'shell'=8] {'pix'}, use_global_device_ids=true, to_apply=%region_3.0 | all-reduce | flops 21 | bytes 168 | tf_op jit(solution)/shard_map/psum | solution.py:45
  271.1 4.1 %multiply_subtract_fusion = f32[20,32768]{1,0:T(8,128)} fusion(f32[20,32768]{1,0:T(8,128)S(1)} %copy-done, s32[20,32768]{1,0:T(8,128)} %param.12, f32[20]{0:T(128)S(1)} %div.29, f32[32768]{0:T(1024)S(1)} %copy-done.3), kind=kLoop, calls=%fused_computation.9 | loop fusion | flops 2621440 | bytes 7995472 | tf_op jit(solution)/shard_map/sub | solution.py:52
  275.8 0.0 collective-permute-done
  275.8 0.0 collective-permute-done.1
  275.8 0.0 collective-permute-done.2
  275.8 0.0 collective-permute-done.3
  275.9 14.8 %fusion.11 = f32[16,32768]{1,0:T(8,128)} fusion(f32[16,32768]{1,0:T(8,128)} %copy-done.1, f32[16,2048]{1,0:T(8,128)} %collective-permute-done.1, f32[16,2048]{1,0:T(8,128)} %collective-permute-done, f32[1,32768]{1,0:T(1,128)} %collective-permute-done.3, f32[1,32768]{1,0:T(1,128)} %collective-permute-done.2, f32[4,20,16]{1,2,0:T(8,128)} %param.10, ...), kind=kOutput, calls=%fused_computation.22 | convolution fusion | flops 516947968 | bytes 7869504 | tf_op jit(solution)/shard_map/dot_general | solution.py:63
  (4 shorter events, 0.0 us)
Async XLA Ops:
  7.2 111.7 %all-reduce.3.cloned.1.call-start = ((), (), s32[]{:S(2)}) async-start(), calls=%async_computation | async-start | bytes 6291456 | tf_op jit(solution)/shard_map/psum | solution.py:44
  10.5 37.9 %copy-start.1 = (f32[16,32768]{1,0:T(8,128)}, f32[16,32768]{1,0:T(8,128)S(1)}, u32[]{:S(2)}) copy-start(f32[16,32768]{1,0:T(8,128)S(1)} %multiply_add_fusion) | copy-start | bytes 6291460
  21.4 11.4 %copy-start.4 = (s32[32768]{0:T(1024)S(1)}, s32[32768]{0:T(1024)}, u32[]{:S(2)}) copy-start(s32[32768]{0:T(1024)} %param.11) | copy-start | bytes 393220
  32.9 0.8 copy-start.2
  41.7 77.2 %copy-start.3 = (f32[32768]{0:T(1024)S(1)}, f32[32768]{0:T(1024)}, u32[]{:S(2)}) copy-start(f32[32768]{0:T(1024)} %param.13) | copy-start | bytes 393220
  41.8 79.6 %copy-start.6 = (f32[16]{0:T(128)S(1)}, f32[16]{0:T(128)}, u32[]{:S(2)}) copy-start(f32[16]{0:T(128)} %param.15) | copy-start | bytes 196
  41.8 150.7 %copy-start.5 = (f32[20]{0:T(128)S(1)}, f32[20]{0:T(128)}, u32[]{:S(2)}) copy-start(f32[20]{0:T(128)} %param.14) | copy-start | bytes 244
  41.8 234.0 %collective-permute-start = (f32[16,2048]{1,0:T(8,128)S(1)}, f32[16,2048]{1,0:T(8,128)}, u32[]{:S(2)}, u32[]{:S(2)}) collective-permute-start(f32[16,2048]{1,0:T(8,128)S(1)} %get-tuple-element.8), channel_id=1, source_target_pairs={{0,8},{8,16},{16,24},{24,32},{32,40},{40,48},{48,56},{56,64},{64,7... | collective-permute-start | bytes 393224 | tf_op jit(solution)/shard_map/ppermute | solution.py:20
  45.4 230.4 %collective-permute-start.1 = (f32[16,2048]{1,0:T(8,128)S(1)}, f32[16,2048]{1,0:T(8,128)}, u32[]{:S(2)}, u32[]{:S(2)}) collective-permute-start(f32[16,2048]{1,0:T(8,128)S(1)} %get-tuple-element.9), channel_id=1, source_target_pairs={{8,0},{16,8},{24,16},{32,24},{40,32},{48,40},{56,48},{64,56},{72,6... | collective-permute-start | bytes 393224 | tf_op jit(solution)/shard_map/ppermute | solution.py:22
  49.3 226.5 %collective-permute-start.2 = (f32[1,32768]{1,0:T(1,128)}, f32[1,32768]{1,0:T(1,128)}, u32[]{:S(2)}, u32[]{:S(2)}) collective-permute-start(f32[1,32768]{1,0:T(1,128)} %get-tuple-element.6), channel_id=1, source_target_pairs={{0,1},{1,2},{2,3},{3,4},{4,5},{5,6},{6,7},{8,9},{9,10},{10,11},{11... | collective-permute-start | bytes 393224 | tf_op jit(solution)/shard_map/ppermute | solution.py:20
  51.3 224.6 %collective-permute-start.3 = (f32[1,32768]{1,0:T(1,128)}, f32[1,32768]{1,0:T(1,128)}, u32[]{:S(2)}, u32[]{:S(2)}) collective-permute-start(f32[1,32768]{1,0:T(1,128)} %get-tuple-element.7), channel_id=1, source_target_pairs={{1,0},{2,1},{3,2},{4,3},{5,4},{6,5},{7,6},{9,8},{10,9},{11,10},{12... | collective-permute-start | bytes 393224 | tf_op jit(solution)/shard_map/ppermute | solution.py:22
  118.9 73.6 %copy-start = (f32[20,32768]{1,0:T(8,128)S(1)}, f32[20,32768]{1,0:T(8,128)}, u32[]{:S(2)}) copy-start(f32[20,32768]{1,0:T(8,128)} %all-reduce.3.cloned.1.call-done) | copy-start | bytes 7864324
Sparse Core Ops, SparseCore 0:
  41.9 76.9 all-reduce.2
where the time goes:
time: 299 us
  blocking collectives  146 us (49%)
  waiting for transfers between devices  66.4 us (22%)
  matrix products  25.7 us (9%)
  other arithmetic  20.8 us (7%)
  between operations  15.9 us (5%)
  local copies, waits for them, and re-layouts  14 us (5%)
  starting transfers between devices  9.87 us (3%)
    psum x2, blocking collectives, shards(): lax.psum((jnp.sum(mask[None, :] * proj, axis=1), jnp.sum(counted, axis=1)...  146 us
    psum x1, waiting for transfers between devices, shards(): proj = lax.psum(partial_proj, 'shell')  66.3 us
    dot_general x1, matrix products, shards(): lax.dot_general(flat, spread, (((0,), (0,)), ((), ())), precision=lax.Pre...  14.8 us
    reshape x1, local copies, waits for them, and re-layouts, shards(): every.reshape(classes, bins, pixels) * onehot[:, None, :]  11.4 us
    dot_general x1, matrix products, shards(): jnp.dot(flat, density, precision=lax.Precision.HIGHEST, preferred_element...  10.9 us
    reduce_sum x1, other arithmetic, shards(): jnp.sum(every.reshape(classes, bins, pixels) * onehot[:, None, :], axis=0)  8.02 us
  transfers between devices with their start and end apart: 5, of which 1 were waited for; matrix products, arithmetic and copies ran while one was open for 4% of the time, Pallas kernels for 0%

commit v1 on v0

--- a/solution.py
+++ b/solution.py
@@ -41,7 +41,10 @@
     )
     partial_proj = jnp.sum(every.reshape(classes, bins, pixels) * onehot[:, None, :], axis=0)
     counted = counts.astype(jnp.float32)
-    proj = lax.psum(partial_proj, "shell")
+    p_count = lax.axis_size("shell")
+    proj = partial_proj
+    for src_i in [[(j0, j0 ^ c) for j0 in range(p_count)] for c in (1, 2, 4, 8, 16) if c < p_count]:
+        proj = proj + lax.ppermute(proj, "shell", src_i)
     weighted, total = lax.psum(
         (jnp.sum(mask[None, :] * proj, axis=1), jnp.sum(counted, axis=1)), "pix"
     )

time: 299 us -> 359 us (1.20)
  waiting for transfers between devices: 66.4 us -> 131 us
  between operations: 15.9 us -> 2.54 us
  starting transfers between devices: 9.87 us -> 14.7 us
    ppermute x0 -> x3, waiting for transfers between devices: none -> 131 us  [shards(): proj = proj + lax.ppermute(proj, 'shell', src_i)]
    psum x1 -> x0, waiting for transfers between devices: 66.3 us -> none  [shards(): proj = lax.psum(partial_proj, 'shell')]
    ppermute x0 -> x3, starting transfers between devices: none -> 4.77 us  [shards(): proj = proj + lax.ppermute(proj, 'shell', src_i)]
  transfers between devices with their start and end apart: 5 -> 7, of which waited for: 1 -> 3; matrix products, arithmetic and copies ran while one was open for 4% -> 4% of each run, Pallas kernels for 0% -> 0%
where the time goes in v1:
time: 359 us
  blocking collectives  149 us (42%)
  waiting for transfers between devices  131 us (36%)
  matrix products  25.6 us (7%)
  other arithmetic  19.8 us (6%)
  local copies, waits for them, and re-layouts  16 us (4%)
  starting transfers between devices  14.7 us (4%)
    psum x2, blocking collectives, shards(): lax.psum((jnp.sum(mask[None, :] * proj, axis=1), jnp.sum(counted, axis=1)...  149 us
    ppermute x3, waiting for transfers between devices, shards(): proj = proj + lax.ppermute(proj, 'shell', src_i)  131 us
    dot_general x1, matrix products, shards(): lax.dot_general(flat, spread, (((0,), (0,)), ((), ())), precision=lax.Pre...  14.8 us
    reshape x1, local copies, waits for them, and re-layouts, shards(): every.reshape(classes, bins, pixels) * onehot[:, None, :]  11.4 us
    dot_general x1, matrix products, shards(): jnp.dot(flat, density, precision=lax.Precision.HIGHEST, preferred_element...  10.9 us
  transfers between devices with their start and end apart: 7, of which 3 were waited for; matrix products, arithmetic and copies ran while one was open for 4% of the time, Pallas kernels for 0%

profile of v1, /device:TPU:8, one launch (start us, length us, event | category | flops | bytes accessed | tf_op | source)
XLA Modules:
  0.0 358.6 jit_solution(10862470013400559715)
XLA Ops:
  0.6 0.8 copy.10
  1.4 0.1 reshape.36
  1.5 2.5 multiply_add_fusion
  3.9 0.0 copy-start.1
  4.0 10.9 %convolution_bitcast_fusion = f32[80,32768]{1,0:T(8,128)} fusion(f32[80,16]{0,1:T(8,128)S(1)} %reshape.36, f32[16,32768]{1,0:T(8,128)S(1)} %multiply_add_fusion), kind=kOutput, calls=%fused_computation | convolution fusion | flops 503316480 | bytes 12588032 | tf_op jit(solution)/shard_map/dot_general | solution.py:39
  14.8 0.0 copy-start.4
  14.8 11.4 %reshape.37 = f32[4,20,32768]{2,1,0:T(8,128)} reshape(f32[80,32768]{1,0:T(8,128)} %convolution_bitcast_fusion) | data formatting | bytes 20971520 | tf_op jit(solution)/shard_map/reshape | solution.py:42
  26.2 0.0 copy-done.4
  26.2 0.1 fusion.22
  26.4 0.0 copy-start.2
  26.4 6.2 %multiply_reduce_fusion = f32[20,32768]{1,0:T(8,128)S(1)} fusion(f32[4,20,32768]{2,1,0:T(8,128)} %reshape.37, f32[4,32768]{1,0:T(4,128)S(1)} %fusion.22), kind=kLoop, calls=%fused_computation.7 | loop fusion | flops 4587520 | bytes 13631488 | tf_op jit(solution)/shard_map/reduce_sum | solution.py:42
  32.6 0.0 copy-done.2
  32.6 0.1 collective-permute-start
  32.7 5.6 %collective-permute-done = f32[20,32768]{1,0:T(8,128)S(1)} collective-permute-done((f32[20,32768]{1,0:T(8,128)S(1)}, f32[20,32768]{1,0:T(8,128)S(1)}, u32[]{:S(2)}, u32[]{:S(2)}) %collective-permute-start) | collective-permute-done | bytes 2621472 | tf_op jit(solution)/shard_map/ppermute | solution.py:47
  38.4 0.4 add.19
  38.8 1.6 collective-permute-start.1
  40.4 0.0 copy-done.1
  40.4 3.5 collective-permute-start.3
  43.9 0.0 copy-start.3
  43.9 3.1 collective-permute-start.4
  47.0 62.0 %collective-permute-done.1 = f32[20,32768]{1,0:T(8,128)S(1)} collective-permute-done((f32[20,32768]{1,0:T(8,128)S(1)}, f32[20,32768]{1,0:T(8,128)S(1)}, u32[]{:S(2)}, u32[]{:S(2)}) %collective-permute-start.1) | collective-permute-done | bytes 2621472 | tf_op jit(solution)/shard_map/ppermute | solution.py:47
  109.0 0.3 add.20
  109.3 3.1 collective-permute-start.2
  112.4 2.4 fusion.23
  114.9 1.9 collective-permute-start.5
  116.8 0.0 copy-start.6
  116.8 0.0 copy-start.5
  116.8 1.4 collective-permute-start.6
  118.2 63.4 %collective-permute-done.2 = f32[20,32768]{1,0:T(8,128)S(1)} collective-permute-done((f32[20,32768]{1,0:T(8,128)S(1)}, f32[20,32768]{1,0:T(8,128)S(1)}, u32[]{:S(2)}, u32[]{:S(2)}) %collective-permute-start.2) | collective-permute-done | bytes 2621472 | tf_op jit(solution)/shard_map/ppermute | solution.py:47
  181.6 0.0 copy-done.3
  181.6 0.0 copy-start
  181.6 0.4 multiply_reduce_fusion.1
  182.1 1.2 copy-done
  183.3 0.0 copy-done.6
  183.3 73.8 %psum.22 = f32[20]{0:T(128)S(1)} all-reduce(f32[20]{0:T(128)S(1)} %multiply_reduce_fusion.1), channel_id=1, replica_groups=mesh['pix'=32,'shell'=8] {'pix'}, use_global_device_ids=true, to_apply=%region_4.0 | all-reduce | flops 20 | bytes 160 | tf_op jit(solution)/shard_map/psum | solution.py:48
  257.1 0.0 copy-done.5
  257.1 4.7 %subtract_reduce_fusion = (f32[]{:T(128)}, f32[20]{0:T(128)S(1)}) fusion(s32[20,32768]{1,0:T(8,128)} %param.12, f32[20]{0:T(128)S(1)} %broadcast_multiply_fusion, f32[20]{0:T(128)S(1)} %copy-done.5, f32[32768]{0:T(1024)S(1)} %copy-done.3, f32[20,32768]{1,0:T(8,128)S(1)} %add.20, f32[20,32768]{1,0:T(8,128)} %copy-done), kind=kLoop, calls=%fused_computation.10 | loop fusion | flops 5898219 | bytes 7995636 | tf_op jit(solution)/shard_map/reduce_sum | solution.py:53
  261.8 75.0 %all-reduce = (f32[20]{0:T(128)S(1)}, f32[]{:T(128)}) all-reduce(f32[20]{0:T(128)S(1)} %get-tuple-element.3, f32[]{:T(128)} %get-tuple-element.2), channel_id=1, replica_groups=mesh['pix'=32,'shell'=8] {'pix'}, use_global_device_ids=true, to_apply=%region_2.0 | all-reduce | flops 21 | bytes 168 | tf_op jit(solution)/shard_map/psum | solution.py:48
  336.8 5.1 %multiply_subtract_fusion = f32[20,32768]{1,0:T(8,128)} fusion(s32[20,32768]{1,0:T(8,128)} %param.12, f32[20]{0:T(128)S(1)} %div.29, f32[32768]{0:T(1024)S(1)} %copy-done.3, f32[20,32768]{1,0:T(8,128)S(1)} %add.20, f32[20,32768]{1,0:T(8,128)} %copy-done), kind=kLoop, calls=%fused_computation.11 | loop fusion | flops 3276800 | bytes 10616912 | tf_op jit(solution)/shard_map/sub | solution.py:55
  342.6 0.0 collective-permute-done.3
  342.6 0.0 collective-permute-done.4
  342.7 0.0 collective-permute-done.5
  342.7 0.0 collective-permute-done.6
  342.7 14.8 %fusion.6 = f32[16,32768]{1,0:T(8,128)} fusion(f32[4,20,16]{1,2,0:T(8,128)} %param.10, f32[20,32768]{1,0:T(8,128)} %multiply_subtract_fusion, f32[4,32768]{1,0:T(4,128)} %copy-done.2, f32[16,32768]{1,0:T(8,128)} %copy-done.1, f32[16,2048]{1,0:T(8,128)} %collective-permute-done.4, f32[16,2048]{1,0:T(8,128)} %collective-permute-done.3, ...), kind=kOutput, calls=%fused_computation.6 | convolution fusion | flops 516947968 | bytes 7869504 | tf_op jit(solution)/shard_map/dot_general | solution.py:66
  (4 shorter events, 0.0 us)
Async XLA Ops:
  3.9 36.4 %copy-start.1 = (f32[16,32768]{1,0:T(8,128)}, f32[16,32768]{1,0:T(8,128)S(1)}, u32[]{:S(2)}) copy-start(f32[16,32768]{1,0:T(8,128)S(1)} %multiply_add_fusion) | copy-start | bytes 6291460
  14.8 11.4 %copy-start.4 = (s32[32768]{0:T(1024)S(1)}, s32[32768]{0:T(1024)}, u32[]{:S(2)}) copy-start(s32[32768]{0:T(1024)} %param.11) | copy-start | bytes 393220
  26.4 6.3 %copy-start.2 = (f32[4,32768]{1,0:T(4,128)}, f32[4,32768]{1,0:T(4,128)S(1)}, u32[]{:S(2)}) copy-start(f32[4,32768]{1,0:T(4,128)S(1)} %fusion.22) | copy-start | bytes 1572868
  32.6 5.7 %collective-permute-start = (f32[20,32768]{1,0:T(8,128)S(1)}, f32[20,32768]{1,0:T(8,128)S(1)}, u32[]{:S(2)}, u32[]{:S(2)}) collective-permute-start(f32[20,32768]{1,0:T(8,128)S(1)} %multiply_reduce_fusion), channel_id=1, source_target_pairs={{0,1},{1,0},{2,3},{3,2},{4,5},{5,4},{6,7},{7,6},{8,9},{9,8},{10,11... | collective-permute-start | bytes 7864328 | tf_op jit(solution)/shard_map/ppermute | solution.py:47
  38.8 70.2 %collective-permute-start.1 = (f32[20,32768]{1,0:T(8,128)S(1)}, f32[20,32768]{1,0:T(8,128)S(1)}, u32[]{:S(2)}, u32[]{:S(2)}) collective-permute-start(f32[20,32768]{1,0:T(8,128)S(1)} %add.19), channel_id=1, source_target_pairs={{0,2},{1,3},{2,0},{3,1},{4,6},{5,7},{6,4},{7,5},{8,10},{9,11},{10,... | collective-permute-start | bytes 7864328 | tf_op jit(solution)/shard_map/ppermute | solution.py:47
  40.4 302.2 %collective-permute-start.3 = (f32[16,2048]{1,0:T(8,128)S(1)}, f32[16,2048]{1,0:T(8,128)}, u32[]{:S(2)}, u32[]{:S(2)}) collective-permute-start(f32[16,2048]{1,0:T(8,128)S(1)} %get-tuple-element.8), channel_id=1, source_target_pairs={{0,8},{8,16},{16,24},{24,32},{32,40},{40,48},{48,56},{56,64},{64,7... | collective-permute-start | bytes 393224 | tf_op jit(solution)/shard_map/ppermute | solution.py:20
  43.9 137.7 %copy-start.3 = (f32[32768]{0:T(1024)S(1)}, f32[32768]{0:T(1024)}, u32[]{:S(2)}) copy-start(f32[32768]{0:T(1024)} %param.13) | copy-start | bytes 393220
  43.9 298.8 %collective-permute-start.4 = (f32[16,2048]{1,0:T(8,128)S(1)}, f32[16,2048]{1,0:T(8,128)}, u32[]{:S(2)}, u32[]{:S(2)}) collective-permute-start(f32[16,2048]{1,0:T(8,128)S(1)} %get-tuple-element.9), channel_id=1, source_target_pairs={{8,0},{16,8},{24,16},{32,24},{40,32},{48,40},{56,48},{64,56},{72,6... | collective-permute-start | bytes 393224 | tf_op jit(solution)/shard_map/ppermute | solution.py:22
  109.3 72.3 %collective-permute-start.2 = (f32[20,32768]{1,0:T(8,128)S(1)}, f32[20,32768]{1,0:T(8,128)S(1)}, u32[]{:S(2)}, u32[]{:S(2)}) collective-permute-start(f32[20,32768]{1,0:T(8,128)S(1)} %add.20), channel_id=1, source_target_pairs={{0,4},{1,5},{2,6},{3,7},{4,0},{5,1},{6,2},{7,3},{8,12},{9,13},{10,... | collective-permute-start | bytes 7864328 | tf_op jit(solution)/shard_map/ppermute | solution.py:47
  114.9 227.8 %collective-permute-start.5 = (f32[1,32768]{1,0:T(1,128)}, f32[1,32768]{1,0:T(1,128)}, u32[]{:S(2)}, u32[]{:S(2)}) collective-permute-start(f32[1,32768]{1,0:T(1,128)} %get-tuple-element.6), channel_id=1, source_target_pairs={{0,1},{1,2},{2,3},{3,4},{4,5},{5,6},{6,7},{8,9},{9,10},{10,11},{11... | collective-permute-start | bytes 393224 | tf_op jit(solution)/shard_map/ppermute | solution.py:20
  116.8 66.5 %copy-start.6 = (f32[16]{0:T(128)S(1)}, f32[16]{0:T(128)}, u32[]{:S(2)}) copy-start(f32[16]{0:T(128)} %param.15) | copy-start | bytes 196
  116.8 140.3 %copy-start.5 = (f32[20]{0:T(128)S(1)}, f32[20]{0:T(128)}, u32[]{:S(2)}) copy-start(f32[20]{0:T(128)} %param.14) | copy-start | bytes 244
  116.8 225.9 %collective-permute-start.6 = (f32[1,32768]{1,0:T(1,128)}, f32[1,32768]{1,0:T(1,128)}, u32[]{:S(2)}, u32[]{:S(2)}) collective-permute-start(f32[1,32768]{1,0:T(1,128)} %get-tuple-element.7), channel_id=1, source_target_pairs={{1,0},{2,1},{3,2},{4,3},{5,4},{6,5},{7,6},{9,8},{10,9},{11,10},{12... | collective-permute-start | bytes 393224 | tf_op jit(solution)/shard_map/ppermute | solution.py:22
  181.6 1.7 copy-start
